TPU v7x, 32 devices: a whole 2x2x4 slice. The times are simulated.
32 devices in a mesh: section: 2 (over y), wide: 8 (over z, core), narrow: 2 (over x).
Axes of the slice: x: 2, y: 2, z: 4, core: 2. Of those that a mesh axis runs over, the one named last changes fastest.
Arguments:
- hidden: bfloat16 [2, 1024, 24576], P('section', None, 'wide'), may hold values from -6 to 6
- down_weight: bfloat16 [12288, 24576], P('narrow', 'wide'), may hold values from -0.0390625 to 0.0390625
- residual: bfloat16 [2, 1024, 12288], P('section', None, 'narrow'), may hold values from -6 to 6
- ln_gain: float32 [12288], P('narrow'), may hold values from 0.5 to 1.5
- ln_bias: float32 [12288], P('narrow'), may hold values from -3 to 3
- qkv_weight: bfloat16 [12288, 24576], P('narrow', 'wide'), may hold values from -1 to 1
Outputs:
- stream: bfloat16 [2, 1024, 12288], P('section', 'wide', 'narrow')
- context: bfloat16 [2, 1024, 8192], P('section', 'narrow', 'wide')
All inputs are finite; a program needn't handle non-finite values.
Results may differ from a plain program's by a relative error of at most 0.007.
Values may be sent and summed in bfloat16 or wider, within the bound.
A program may use at most 320 MiB of HBM per device.

v0:
```python
import jax
import jax.numpy as jnp
from jax import lax
from jax.sharding import PartitionSpec as P

D = 12288
HDIM = 128


def from_behind(value, axis, steps):
    count = lax.axis_size(axis)
    pairs = [(source, (source + steps) % count) for source in range(count)]
    return lax.ppermute(value, axis, pairs)


def per_device(hidden, down_weight, residual, ln_gain, ln_bias, qkv_weight):
    inner = hidden[0]
    resid = residual[0]
    seq_len = inner.shape[0]
    wide_rows = seq_len // lax.axis_size("wide")
    wide_at = lax.axis_index("wide")
    contract = (((1,), (1,)), ((), ()))
    partial_ffn = lax.dot_general(inner, down_weight, contract, preferred_element_type=jnp.float32)
    summed = lax.psum(partial_ffn, "wide")
    mine = (resid.astype(jnp.float32) + summed).astype(jnp.bfloat16)
    arrived = from_behind(mine, "section", 1)
    own_rows = lax.dynamic_slice_in_dim(mine, wide_at * wide_rows, wide_rows, 0)
    values = arrived.astype(jnp.float32)
    totals, squares = lax.psum(
        (jnp.sum(values, axis=1), jnp.sum(values * values, axis=1)), "narrow"
    )
    mean = totals / D
    var = squares / D - mean * mean
    normed = (
        (values - mean[:, None]) * lax.rsqrt(var + 1e-05)[:, None] * ln_gain + ln_bias
    ).astype(jnp.bfloat16)
    heads_here = qkv_weight.shape[1] // (3 * HDIM)
    query_count = seq_len // lax.axis_size("narrow")
    narrow_at = lax.axis_index("narrow")
    joined = lax.psum(
        jnp.dot(normed, qkv_weight, preferred_element_type=jnp.float32), "narrow"
    ).astype(jnp.bfloat16)
    mine_joined = lax.dynamic_slice_in_dim(joined, narrow_at * query_count, query_count, 0)
    query = mine_joined.reshape(query_count, heads_here, 3, HDIM)[:, :, 0]
    pairs = joined.reshape(seq_len, heads_here, 3, HDIM)[:, :, 1:]
    keys = pairs[:, :, 0]
    vals = pairs[:, :, 1]
    scores = jnp.einsum("qhd,khd->hqk", query, keys, preferred_element_type=jnp.float32) / jnp.sqrt(
        jnp.float32(HDIM)
    )
    query_pos = narrow_at * query_count + lax.broadcasted_iota(jnp.int32, (query_count, seq_len), 0)
    key_pos = lax.broadcasted_iota(jnp.int32, (query_count, seq_len), 1)
    scores = jnp.where((key_pos <= query_pos)[None], scores, jnp.float32(-1e30))
    top = jnp.max(scores, axis=2, keepdims=True)
    expd = jnp.exp(scores - top)
    probs = (expd / jnp.sum(expd, axis=2, keepdims=True)).astype(jnp.bfloat16)
    attended = jnp.einsum("hqk,khd->qhd", probs, vals, preferred_element_type=jnp.float32).astype(
        jnp.bfloat16
    )
    attended = attended.reshape(query_count, heads_here * HDIM)
    return (own_rows[None], attended[None])


def solution(mesh):
    return jax.shard_map(
        per_device,
        mesh=mesh,
        in_specs=(
            P("section", None, "wide"),
            P("narrow", "wide"),
            P("section", None, "narrow"),
            P("narrow"),
            P("narrow"),
            P("narrow", "wide"),
        ),
        out_specs=(P("section", "wide", "narrow"), P("section", "narrow", "wide")),
        check_vma=False,
    )
```

profile of v0, /device:TPU:0, one launch (start us, length us, event | category | flops | bytes accessed | tf_op | source)
XLA Modules:
  0.0 1245.0 jit_solution(1324470787373891507)
XLA Ops:
  7.2 0.0 all-reduce.4.cloned.1.call-start
  7.2 46.9 %fusion.18 = f32[1024,6144]{1,0:T(8,128)} fusion(bf16[6144,3072]{1,0:T(8,128)(2,1)} %param.7, bf16[1,1024,3072]{2,1,0:T(8,128)(2,1)} %param.6), kind=kOutput, calls=%fused_computation.24 | convolution fusion | flops 38654705664 | bytes 69206016 | tf_op jit(solution)/shard_map/dot_general | solution.py:23
  54.1 0.0 all-reduce.4.cloned.1.call-update
  54.1 0.0 copy-start.1
  54.1 0.0 copy-start.2
  54.1 493.4 %all-reduce.4.cloned.1.call-done = f32[1024,6144]{1,0:T(8,128)} async-done(((f32[1024,6144]{1,0:T(8,128)}), f32[1024,6144]{1,0:T(8,128)}) %all-reduce.4.cloned.1.call-update) | async-done | bytes 25165840 | tf_op jit(solution)/shard_map/psum | solution.py:24
  547.5 17.2 %fusion.6 = bf16[1024,6144]{1,0:T(8,128)(2,1)} fusion(f32[1024,6144]{1,0:T(8,128)} %all-reduce.4.cloned.1.call-done, bf16[1,1024,6144]{2,1,0:T(8,128)(2,1)} %param.8), kind=kLoop, calls=%fused_computation.10 | loop fusion | flops 18874368 | bytes 50331648 | tf_op jit(solution)/shard_map/convert_element_type | solution.py:25
  564.7 1.5 collective-permute-start
  566.1 1.2 iota_compare_fusion
  567.3 2.7 dynamic-slice_bitcast_fusion
  570.0 266.8 %collective-permute-done = bf16[1024,6144]{1,0:T(8,128)(2,1)} collective-permute-done((bf16[1024,6144]{1,0:T(8,128)(2,1)}, bf16[1024,6144]{1,0:T(8,128)(2,1)}, u32[]{:S(2)}, u32[]{:S(2)}) %collective-permute-start) | collective-permute-done | bytes 12582944 | tf_op jit(solution)/shard_map/ppermute | solution.py:13
  836.8 8.5 convert_reduce_fusion
  845.3 5.0 all-reduce
  850.3 0.0 copy-done.1
  850.3 0.0 copy-done.2
  850.3 48.3 %fusion.8 = f32[1024,3072]{1,0:T(8,128)} fusion(bf16[6144,3072]{1,0:T(8,128)(2,1)} %param.11, bf16[1024,6144]{1,0:T(8,128)(2,1)} %collective-permute-done, f32[6144]{0:T(1024)S(1)} %copy-done.1, f32[6144]{0:T(1024)S(1)} %copy-done.2, f32[1024]{0:T(1024)S(1)} %get-tuple-element.11, f32[1024]{0:T(1024)S(1)} %get-tuple-element.10), kind=kOutput, calls=%fused_computation.15 | convolution fusion | flops 38692454400 | bytes 62971904 | tf_op jit(solution)/shard_map/dot_general | solution.py:41
  898.6 285.4 %all-reduce.5 = bf16[1024,3072]{1,0:T(8,128)(2,1)} all-reduce(f32[1024,3072]{1,0:T(8,128)} %fusion.8), channel_id=1, replica_groups=mesh['section'=2,'wide'=8,'narrow'=2] {'narrow'}, use_global_device_ids=true, to_apply=%region_5.0 | all-reduce | flops 3145728 | bytes 18874368 | tf_op jit(solution)/shard_map/psum | solution.py:40
  1184.0 8.6 copy.11
  1192.6 2.1 constant_dynamic-slice_fusion
  1194.7 2.8 copy.13
  1197.5 10.1 fusion.20
  1207.6 21.2 %fusion.24 = (f32[8,512]{1,0:T(8,128)S(1)}, f32[8,512,1024]{2,1,0:T(8,128)}) fusion(f32[8,512,1024]{2,1,0:T(8,128)} %fusion.20, pred[512,1024]{1,0:T(8,128)(4,1)S(1)} %copy-done), kind=kOutput, calls=%fused_computation.39 | output fusion | flops 25166848 | bytes 34095104 | tf_op jit(solution)/shard_map/sub | solution.py:55
  1228.8 8.0 fusion.21
  1236.9 1.3 copy.16
  (4 shorter events, 0.0 us)
Async XLA Ops:
  7.2 540.3 %all-reduce.4.cloned.1.call-start = ((), (), s32[]{:S(2)}) async-start(), calls=%async_computation | async-start | bytes 50331648 | tf_op jit(solution)/shard_map/psum | solution.py:24
  54.1 796.2 %copy-start.1 = (f32[6144]{0:T(1024)S(1)}, f32[6144]{0:T(1024)}, u32[]{:S(2)}) copy-start(f32[6144]{0:T(1024)} %param.10) | copy-start | bytes 73732
  54.1 796.2 %copy-start.2 = (f32[6144]{0:T(1024)S(1)}, f32[6144]{0:T(1024)}, u32[]{:S(2)}) copy-start(f32[6144]{0:T(1024)} %param.9) | copy-start | bytes 73732
  564.7 272.1 %collective-permute-start = (bf16[1024,6144]{1,0:T(8,128)(2,1)}, bf16[1024,6144]{1,0:T(8,128)(2,1)}, u32[]{:S(2)}, u32[]{:S(2)}) collective-permute-start(bf16[1024,6144]{1,0:T(8,128)(2,1)} %fusion.6), channel_id=1, source_target_pairs={{0,16},{16,0},{1,17},{17,1},{2,18},{18,2},{3,19},{19,3},{4,20},{20... | collective-permute-start | bytes 37748744 | tf_op jit(solution)/shard_map/ppermute | solution.py:13
  1197.5 10.1 copy-start
Sparse Core Ops, SparseCore 0:
  54.2 493.2 all-reduce.3
where the time goes:
time: 1250 us
  waiting for transfers between devices  760 us (61%)
  blocking collectives  290 us (23%)
  matrix products  113 us (9%)
  other arithmetic  48.1 us (4%)
  local copies, waits for them, and re-layouts  17.6 us (1%)
  between operations  14.1 us (1%)
    psum x1, waiting for transfers between devices, per_device(): summed = lax.psum(partial_ffn, 'wide')  493 us
    psum x1, blocking collectives, per_device(): lax.psum(jnp.dot(normed, qkv_weight, preferred_element_type=jnp.float32),...  285 us
    ppermute x1, waiting for transfers between devices, from_behind(): return lax.ppermute(value, axis, pairs)  267 us
    dot_general x1, matrix products, per_device(): jnp.dot(normed, qkv_weight, preferred_element_type=jnp.float32)  48.3 us
    dot_general x1, matrix products, per_device(): lax.dot_general(inner, down_weight, contract, preferred_element_type=jnp....  46.9 us
  transfers between devices with their start and end apart: 2, of which 2 were waited for; matrix products, arithmetic and copies ran while one was open for 0% of the time, Pallas kernels for 0%

commit v1 on v0

--- a/solution.py
+++ b/solution.py
@@ -21,7 +21,12 @@
     wide_at = lax.axis_index("wide")
     contract = (((1,), (1,)), ((), ()))
     partial_ffn = lax.dot_general(inner, down_weight, contract, preferred_element_type=jnp.float32)
-    summed = lax.psum(partial_ffn, "wide")
+
+    def _switch_orders(x_local):
+        last = jnp.sum(lax.all_gather(x_local, "wide"), axis=0)
+        return last
+
+    summed = _switch_orders(partial_ffn)
     mine = (resid.astype(jnp.float32) + summed).astype(jnp.bfloat16)
     arrived = from_behind(mine, "section", 1)
     own_rows = lax.dynamic_slice_in_dim(mine, wide_at * wide_rows, wide_rows, 0)

time: 1250 us -> 2490 us (1.99)
  waiting for transfers between devices: 760 us -> 1940 us
  other arithmetic: 48.1 us -> 118 us
    all_gather x0 -> x1, waiting for transfers between devices: none -> 1670 us  [_switch_orders(): last = jnp.sum(lax.all_gather(x_local, 'wide'), axis=0)]
    psum x1 -> x0, waiting for transfers between devices: 493 us -> none  [per_device(): summed = lax.psum(partial_ffn, 'wide')]
    reduce_sum x0 -> x1, other arithmetic: none -> 70.2 us  [_switch_orders(): last = jnp.sum(lax.all_gather(x_local, 'wide'), axis=0)]
where the time goes in v1:
time: 2490 us
  waiting for transfers between devices  1940 us (78%)
  blocking collectives  291 us (12%)
  other arithmetic  118 us (5%)
  matrix products  113 us (5%)
    all_gather x1, waiting for transfers between devices, _switch_orders(): last = jnp.sum(lax.all_gather(x_local, 'wide'), axis=0)  1670 us
    psum x1, blocking collectives, per_device(): lax.psum(jnp.dot(normed, qkv_weight, preferred_element_type=jnp.float32),...  286 us
    ppermute x1, waiting for transfers between devices, from_behind(): return lax.ppermute(value, axis, pairs)  267 us
    reduce_sum x1, other arithmetic, _switch_orders(): last = jnp.sum(lax.all_gather(x_local, 'wide'), axis=0)  70.2 us
  transfers between devices with their start and end apart: 2, of which 2 were waited for; matrix products, arithmetic and copies ran while one was open for 0% of the time, Pallas kernels for 0%

profile of v1, /device:TPU:0, one launch (start us, length us, event | category | flops | bytes accessed | tf_op | source)
XLA Modules:
  0.0 2491.5 jit_solution(4011111177427958687)
XLA Ops:
  7.2 0.0 all-gather.3.cloned.1.call-start
  7.2 46.8 %fusion.18 = f32[1024,6144]{1,0:T(8,128)} fusion(bf16[6144,3072]{1,0:T(8,128)(2,1)} %param.7, bf16[1,1024,3072]{2,1,0:T(8,128)(2,1)} %param.6), kind=kOutput, calls=%fused_computation.24 | convolution fusion | flops 38654705664 | bytes 69206016 | tf_op jit(solution)/shard_map/dot_general | solution.py:23
  54.0 0.0 all-gather.3.cloned.1.call-update
  54.0 1668.3 %all-gather.3.cloned.1.call-done = f32[8192,6144]{1,0:T(8,128)} async-done(((f32[1024,6144]{1,0:T(8,128)}), f32[8192,6144]{1,0:T(8,128)}) %all-gather.3.cloned.1.call-update) | async-done | bytes 201326608 | tf_op jit(solution)/shard_map/all_gather | solution.py:26
  1722.3 70.2 %reduce_sum.36 = f32[1024,6144]{1,0:T(8,128)} reduce(f32[8,1024,6144]{2,1,0:T(8,128)} %bitcast.2, f32[]{:T(128)} %constant.12.clone.1), dimensions={0}, to_apply=%region_0.0 | reduce | flops 44040192 | bytes 226492416 | tf_op jit(solution)/shard_map/reduce_sum | solution.py:26
  1792.5 17.1 fusion.6
  1809.6 1.5 collective-permute-start
  1811.1 1.2 iota_compare_fusion
  1812.3 2.7 dynamic-slice_bitcast_fusion
  1815.0 267.5 %collective-permute-done = bf16[1024,6144]{1,0:T(8,128)(2,1)} collective-permute-done((bf16[1024,6144]{1,0:T(8,128)(2,1)}, bf16[1024,6144]{1,0:T(8,128)(2,1)}, u32[]{:S(2)}, u32[]{:S(2)}) %collective-permute-start) | collective-permute-done | bytes 12582944 | tf_op jit(solution)/shard_map/ppermute | solution.py:13
  2082.5 8.5 convert_reduce_fusion
  2090.9 5.0 all-reduce
  2096.0 0.0 copy-done.1
  2096.0 0.0 copy-done.2
  2096.0 48.2 %fusion.8 = f32[1024,3072]{1,0:T(8,128)} fusion(bf16[6144,3072]{1,0:T(8,128)(2,1)} %param.11, bf16[1024,6144]{1,0:T(8,128)(2,1)} %collective-permute-done, f32[6144]{0:T(1024)S(1)} %copy-done.1, f32[6144]{0:T(1024)S(1)} %copy-done.2, f32[1024]{0:T(1024)S(1)} %get-tuple-element.11, f32[1024]{0:T(1024)S(1)} %get-tuple-element.10), kind=kOutput, calls=%fused_computation.15 | convolution fusion | flops 38692454400 | bytes 62971904 | tf_op jit(solution)/shard_map/dot_general | solution.py:46
  2144.1 286.4 %all-reduce.2 = bf16[1024,3072]{1,0:T(8,128)(2,1)} all-reduce(f32[1024,3072]{1,0:T(8,128)} %fusion.8), channel_id=1, replica_groups=mesh['section'=2,'wide'=8,'narrow'=2] {'narrow'}, use_global_device_ids=true, to_apply=%region_5.0 | all-reduce | flops 3145728 | bytes 18874368 | tf_op jit(solution)/shard_map/psum | solution.py:45
  2430.5 8.6 copy.11
  2439.1 2.1 constant_dynamic-slice_fusion
  2441.2 2.8 copy.13
  2444.1 10.0 fusion.20
  2454.1 0.0 copy-done
  2454.1 21.2 fusion.24
  2475.3 8.0 fusion.21
  2483.4 1.3 copy.16
  (5 shorter events, 0.0 us)
Async XLA Ops:
  7.2 1715.2 %all-gather.3.cloned.1.call-start = ((), (), s32[]{:S(2)}) async-start(), calls=%async_computation | async-start | bytes 226492416 | tf_op jit(solution)/shard_map/all_gather | solution.py:26
  1792.5 303.4 %copy-start.1 = (f32[6144]{0:T(1024)S(1)}, f32[6144]{0:T(1024)}, u32[]{:S(2)}) copy-start(f32[6144]{0:T(1024)} %param.10) | copy-start | bytes 73732
  1792.5 303.4 %copy-start.2 = (f32[6144]{0:T(1024)S(1)}, f32[6144]{0:T(1024)}, u32[]{:S(2)}) copy-start(f32[6144]{0:T(1024)} %param.9) | copy-start | bytes 73732
  1809.6 272.8 %collective-permute-start = (bf16[1024,6144]{1,0:T(8,128)(2,1)}, bf16[1024,6144]{1,0:T(8,128)(2,1)}, u32[]{:S(2)}, u32[]{:S(2)}) collective-permute-start(bf16[1024,6144]{1,0:T(8,128)(2,1)} %fusion.6), channel_id=1, source_target_pairs={{0,16},{16,0},{1,17},{17,1},{2,18},{18,2},{3,19},{19,3},{4,20},{20... | collective-permute-start | bytes 37748744 | tf_op jit(solution)/shard_map/ppermute | solution.py:13
  2444.1 10.1 copy-start
Sparse Core Ops, SparseCore 0:
  54.1 1668.1 all-gather.2
